TPU v7x, 256 devices: a whole 4x4x8 slice. The times are simulated.
256 devices in a mesh: replica: 32 (over y, z_lo, core), fsdp: 8 (over x, z_hi).
Axes of the slice: x: 4, y: 4, z: 8 (z_hi: 2, z_lo: 4; z = z_hi * 4 + z_lo), core: 2. Of those that a mesh axis runs over, the one named last changes fastest.
Arguments:
- tokens: bfloat16 [98304, 8192], P(('replica', 'fsdp')), may hold values from -6 to 6
- inner_weight: bfloat16 [32, 8192, 512], P('replica', 'fsdp'), may hold values from -0.0625 to 0.0625
- cotangent: bfloat16 [98304, 512], P(('replica', 'fsdp')), may hold values from -0.059814453 to 0.059814453
- local_weights: bfloat16 [32, 2, 8192, 896], P('replica', None, 'fsdp'), may hold values from -3 to 3
- anchor: bfloat16 [2, 8, 1024, 896], P(None, 'fsdp', 'replica'), may hold values from -1.5 to 1.5
- momentum: float32 [2, 8, 1024, 896], P(None, 'fsdp', 'replica'), may hold values from -1.5 to 1.5
Outputs:
- keys: bfloat16 [98304, 512], P(('replica', 'fsdp'))
- weight_grad: bfloat16 [32, 8192, 512], P('replica', 'fsdp')
- new_weights: bfloat16 [2, 8192, 896], P(None, 'fsdp')
- new_momentum: float32 [2, 8, 1024, 896], P(None, 'fsdp', 'replica')
All inputs are finite; a program needn't handle non-finite values.
Results may differ from a plain program's by a relative error of at most 0.017.
Values may be sent and summed in bfloat16 or wider, within the bound.
A program may use at most 128 MiB of HBM per device.

v0:
```python
import jax
import jax.numpy as jnp
from jax import lax
from jax.sharding import PartitionSpec as P

outer_rate = 0.7
momentum_decay = 0.9


def outer_step(local_weights, anchor, momentum):
    workers = lax.axis_size("replica")
    local_slab = local_weights[0].astype(jnp.float32)
    summed = lax.psum_scatter(local_slab, "replica", scatter_dimension=1, tiled=True)
    average = summed / workers
    anchor_now = anchor[:, 0].astype(jnp.float32)
    pseudo_grad = anchor_now - average
    momentum_new = momentum_decay * momentum[:, 0] + pseudo_grad
    new_piece = (anchor_now - outer_rate * (pseudo_grad + momentum_decay * momentum_new)).astype(
        jnp.bfloat16
    )
    gathered = lax.all_gather(new_piece, "replica", axis=1, tiled=True)
    return (gathered, momentum_new[:, None])


def inner_pass(tokens, inner_weight, cotangent):
    weight = inner_weight[0]
    columns = tokens
    key_rows = jnp.dot(
        columns,
        lax.all_gather(weight, "fsdp", axis=0, tiled=True),
        preferred_element_type=jnp.float32,
    ).astype(jnp.bfloat16)
    columns = tokens
    grad_sum = lax.psum_scatter(
        lax.dot_general(
            columns, cotangent, (((0,), (0,)), ((), ())), preferred_element_type=jnp.float32
        ).astype(jnp.bfloat16),
        "fsdp",
        scatter_dimension=0,
        tiled=True,
    )
    return (key_rows, grad_sum[None])


def shards(tokens, inner_weight, cotangent, local_weights, anchor, momentum):
    new_weights, new_momentum = outer_step(local_weights, anchor, momentum)
    keys, weight_grad = inner_pass(tokens, inner_weight, cotangent)
    return (keys, weight_grad, new_weights, new_momentum)


def solution(mesh):
    return jax.shard_map(
        shards,
        mesh=mesh,
        in_specs=(
            P(("replica", "fsdp"), None),
            P("replica", "fsdp", None),
            P(("replica", "fsdp"), None),
            P("replica", None, "fsdp", None),
            P(None, "fsdp", "replica", None),
            P(None, "fsdp", "replica", None),
        ),
        out_specs=(
            P(("replica", "fsdp"), None),
            P("replica", "fsdp", None),
            P(None, "fsdp", None),
            P(None, "fsdp", "replica", None),
        ),
        check_vma=False,
    )
```

profile of v0, /device:TPU:7, one launch (start us, length us, event | category | flops | bytes accessed | tf_op | source)
XLA Modules:
  0.0 540.2 jit_solution(11902919102617137104)
XLA Ops:
  8.0 0.0 copy-start
  8.0 0.0 reduce-scatter.5.cloned.1.call-start
  8.1 5.6 %bitcast_convert_fusion = f32[2,1024,896]{2,1,0:T(8,128)} fusion(bf16[1,2,1024,896]{3,2,1,0:T(8,128)(2,1)} %param.9), kind=kLoop, calls=%fused_computation.3 | loop fusion | flops 1835008 | bytes 11010048 | tf_op jit(solution)/shard_map/convert_element_type | solution.py:12
  13.6 0.0 copy-start.1
  13.6 0.0 copy-start.2
  13.6 0.0 reduce-scatter.5.cloned.1.call-update
  13.6 0.0 all-gather.6.cloned.1.call-start
  13.7 0.5 all-gather.6.cloned.1.call-update
  14.2 0.0 all-gather.4.cloned.1.call-start
  14.3 262.2 %reduce-scatter.5.cloned.1.call-done = f32[2,32,896]{2,1,0:T(8,128)} async-done(((f32[2,1024,896]{2,1,0:T(8,128)}), f32[2,32,896]{2,1,0:T(8,128)}) %reduce-scatter.5.cloned.1.call-update) | async-done | bytes 229392 | tf_op jit(solution)/shard_map/reduce_scatter | solution.py:13
  276.5 0.0 copy-done.1
  276.5 0.0 copy-done.2
  276.5 1.7 fusion.6
  278.3 0.0 all-gather.4.cloned.1.call-update
  278.3 0.0 reduce-scatter.3.cloned.1.call-start
  278.3 0.0 copy-done
  278.3 9.6 %convolution_convert_fusion = bf16[8192,512]{1,0:T(8,128)(2,1)} fusion(bf16[384,8192]{1,0:T(8,128)(2,1)} %param.6, bf16[384,512]{1,0:T(8,128)(2,1)S(1)} %copy-done), kind=kOutput, calls=%fused_computation | convolution fusion | flops 3225419776 | bytes 15073280 | tf_op jit(solution)/shard_map/dot_general | solution.py:35
  288.0 0.0 reduce-scatter.3.cloned.1.call-update
  288.0 0.0 all-gather.6.cloned.1.call-done
  288.0 9.4 %fusion.2 = bf16[384,512]{1,0:T(8,128)(2,1)} fusion(bf16[384,8192]{1,0:T(8,128)(2,1)} %param.6, bf16[1,8192,512]{2,1,0:T(8,128)(2,1)} %all-gather.6.cloned.1.call-done), kind=kOutput, calls=%fused_computation.4 | convolution fusion | flops 3221422080 | bytes 15073280 | tf_op jit(solution)/shard_map/dot_general | solution.py:28
  297.4 47.9 %all-gather.4.cloned.1.call-done = bf16[2,1024,896]{2,1,0:T(8,128)(2,1)} async-done(((bf16[2,32,896]{2,1,0:T(8,128)(2,1)}), bf16[2,1024,896]{2,1,0:T(8,128)(2,1)}) %all-gather.4.cloned.1.call-update) | async-done | bytes 3670032 | tf_op jit(solution)/shard_map/all_gather | solution.py:21
  345.3 183.2 %reduce-scatter.3.cloned.1.call-done = bf16[1024,512]{1,0:T(8,128)(2,1)} async-done(((bf16[8192,512]{1,0:T(8,128)(2,1)}), bf16[1024,512]{1,0:T(8,128)(2,1)}) %reduce-scatter.3.cloned.1.call-update) | async-done | bytes 1048592 | tf_op jit(solution)/shard_map/reduce_scatter | solution.py:34
  528.4 4.2 copy.13
Async XLA Ops:
  8.0 270.3 %copy-start = (bf16[384,512]{1,0:T(8,128)(2,1)S(1)}, bf16[384,512]{1,0:T(8,128)(2,1)}, u32[]{:S(2)}) copy-start(bf16[384,512]{1,0:T(8,128)(2,1)} %param.8) | copy-start | bytes 1179652
  8.0 268.5 %reduce-scatter.5.cloned.1.call-start = ((), (), s32[]{:S(2)}) async-start(), calls=%async_computation.3 | async-start | bytes 7569408 | tf_op jit(solution)/shard_map/reduce_scatter | solution.py:13
  13.6 262.9 %copy-start.1 = (f32[2,1,32,896]{3,2,1,0:T(8,128)S(1)}, f32[2,1,32,896]{3,2,1,0:T(8,128)}, u32[]{:S(2)}) copy-start(f32[2,1,32,896]{3,2,1,0:T(8,128)} %param.11) | copy-start | bytes 688132
  13.6 262.9 %copy-start.2 = (bf16[2,1,32,896]{3,2,1,0:T(8,128)(2,1)S(1)}, bf16[2,1,32,896]{3,2,1,0:T(8,128)(2,1)}, u32[]{:S(2)}) copy-start(bf16[2,1,32,896]{3,2,1,0:T(8,128)(2,1)} %param.10) | copy-start | bytes 344068
  13.6 274.4 %all-gather.6.cloned.1.call-start = ((), (), s32[]{:S(2)}) async-start(), calls=%async_computation.5 | async-start | bytes 9437184 | tf_op jit(solution)/shard_map/all_gather | solution.py:30
  14.2 331.0 %all-gather.4.cloned.1.call-start = ((), (), s32[]{:S(2)}) async-start(), calls=%async_computation.4 | async-start | bytes 3784704 | tf_op jit(solution)/shard_map/all_gather | solution.py:21
  278.3 250.2 %reduce-scatter.3.cloned.1.call-start = ((), (), s32[]{:S(2)}) async-start(), calls=%async_computation.2 | async-start | bytes 9437184 | tf_op jit(solution)/shard_map/reduce_scatter | solution.py:34
Sparse Core Ops, SparseCore 0:
  13.8 262.7 reduce-scatter.4
Sparse Core Ops, SparseCore 1:
  16.8 142.0 all-gather.5
  278.4 66.8 all-gather.3
  349.9 178.5 reduce-scatter.2
where the time goes:
time: 542 us; the launch traced here: 540 us
  waiting for transfers between devices  494 us (91%)
  matrix products  19 us (4%)
  between operations  15.7 us (3%)
  other arithmetic  7.29 us (1%)
    reduce_scatter x1, waiting for transfers between devices, outer_step(): lax.psum_scatter(local_slab, 'replica', scatter_dimension=1, tiled=True)  262 us
    reduce_scatter x1, waiting for transfers between devices, inner_pass(): lax.psum_scatter(lax.dot_general(columns, cotangent, (((0,), (0,)), ((),...  183 us
    all_gather x1, waiting for transfers between devices, outer_step(): gathered = lax.all_gather(new_piece, 'replica', axis=1, tiled=True)  47.9 us
  transfers between devices with their start and end apart: 4, of which 3 were waited for; matrix products, arithmetic and copies ran while one was open for 4% of the time, Pallas kernels for 0%

commit v1 on v0

v1 whole, which is shorter than its diff:
```python
import jax
import jax.numpy as jnp
from jax import lax
from jax.experimental import pallas as pl
from jax.experimental.pallas import tpu as pltpu
from jax.sharding import PartitionSpec as P

outer_rate = 0.7
momentum_decay = 0.9
MESH = pl.DeviceIdType.MESH
F32 = jnp.float32
BF16 = jnp.bfloat16

X, Y, ZL = 4, 4, 4
TOK, SLAB, KW = 384, 1024, 512
ROWS, KV = 32, 896
WCH = 4
GCH = 4
LAST_W = 1

L_, W_, C_, TO, TN, YR, ZR, ZG, YG, CG, G_, K_ = (0, 2, 6, 9, 12, 15, 18, 21, 24, 27, 28, 32)
NSEM = 35


def kernel(tok, wgt, cot, loc, anc, mom, keys, wgrad, neww, newm,
           tbuf, cbuf, wbuf, lown, lrecv, s1, s1r, s2, s2f, s2r, ancv, momv, piece, momo,
           kacc, ksend, krecv, kout, gsend, grecv, gown, gout, ss, rs, ls, os):
    r = lax.axis_index("replica")
    f = lax.axis_index("fsdp")
    y, zl, c = r // 8, (r // 2) % 4, r % 2
    x, zh = f // 2, f % 2

    def at_x(k):
        return (r, lax.rem(x + k, X) * 2 + zh)

    def at_y(k):
        return (lax.rem(y + k, Y) * 8 + zl * 2 + c, f)

    def at_z(k):
        return (y * 8 + lax.rem(zl + k, ZL) * 2 + c, f)

    across = (r, x * 2 + (1 - zh))
    sibling = (y * 8 + zl * 2 + (1 - c), f)

    barrier = pltpu.get_barrier_semaphore()
    peers = [across, sibling]
    for k in (1, 2, 3):
        peers += [at_x(k), at_y(k), at_z(k)]
    for p in peers:
        pl.semaphore_signal(barrier, inc=1, device_id=p, device_id_type=MESH)

    def load(i, src, dst):
        cp = pltpu.make_async_copy(src, dst, ls.at[i])
        cp.start()
        return cp

    def column(who, half):
        return pl.ds(pl.multiple_of((who * 2 + half) * SLAB, SLAB), SLAB)

    ld_l = [load(m, loc.at[m, :, :, c], lown.at[m]) for m in range(2)]
    ld_a = load(2, anc, ancv)
    ld_m = load(3, mom, momv)
    ld_c = load(4, cot, cbuf.at[pl.ds(0, TOK)])
    ld_to = load(5, tok.at[:, column(x, 1 - zh)], tbuf.at[0, pl.ds(0, TOK)])
    ld_tn = load(6, tok.at[:, column(x, zh)], tbuf.at[1, pl.ds(0, TOK)])
    ld_w = load(7, wgt, wbuf.at[1])

    pl.semaphore_wait(barrier, len(peers))

    def send(i, src, dst, to):
        cp = pltpu.make_async_remote_copy(
            src_ref=src, dst_ref=dst, send_sem=ss.at[i], recv_sem=rs.at[i],
            device_id=to, device_id_type=MESH)
        cp.start()
        return cp

    def send_w(j):
        rows = pl.ds(j * (SLAB // WCH), SLAB // WCH)
        return send(W_ + j, wgt.at[rows], wbuf.at[0, rows], across)

    c_l = [send(L_ + m, loc.at[m, :, :, 1 - c], lrecv.at[m], sibling) for m in range(2)]
    c_w = [send_w(j) for j in range(WCH - LAST_W)]
    c_c = [send(C_ + k - 1, cot, cbuf.at[pl.ds(k * TOK, TOK)], at_x(k)) for k in (1, 3, 2)]
    c_to = [send(TO + k - 1, tok.at[:, column(lax.rem(x + k, X), 1 - zh)],
                 tbuf.at[0, pl.ds(k * TOK, TOK)], at_x(k)) for k in (1, 3, 2)]
    c_tn = [send(TN + k - 1, tok.at[:, column(lax.rem(x + k, X), zh)],
                 tbuf.at[1, pl.ds(k * TOK, TOK)], at_x(k)) for k in (1, 3, 2)]

    for m in range(2):
        ld_l[m].wait()
        c_l[m].wait_recv()

        @pl.loop(0, Y * ZL)
        def _(i):
            a, b = i // ZL, i % ZL
            s1[m, a, b] = (lown[m, a, b].astype(F32) + lrecv[m, a, b].astype(F32)).astype(BF16)

    c_y = [send(YR + k - 1, s1.at[:, lax.rem(y + k, Y)], s1r.at[k - 1], at_y(k)) for k in (1, 3, 2)]
    for cp in c_y:
        cp.wait_recv()

    @pl.loop(0, 2 * ZL)
    def _(i):
        m, b = i // ZL, i % ZL
        total = lown[m, y, b].astype(F32) + lrecv[m, y, b].astype(F32)
        for k in range(3):
            total += s1r[k, m, b].astype(F32)
        s2f[m, b] = total
        s2[m, b] = total.astype(BF16)

    c_z = [send(ZR + k - 1, s2.at[:, lax.rem(zl + k, ZL)], s2r.at[k - 1], at_z(k)) for k in (1, 3, 2)]
    c_w += [send_w(j) for j in range(WCH - LAST_W, WCH)]
    ld_a.wait()
    ld_m.wait()
    for cp in c_z:
        cp.wait_recv()

    @pl.loop(0, 2)
    def _(m):
        total = s2f[m, zl]
        for k in range(3):
            total += s2r[k, m].astype(F32)
        anchor_now = ancv[m].astype(F32)
        pseudo = anchor_now - total / 32.0
        momentum_new = momentum_decay * momv[m] + pseudo
        momo[m] = momentum_new
        piece[m] = (anchor_now - outer_rate * (pseudo + momentum_decay * momentum_new)).astype(BF16)

    def store(i, src, dst):
        cp = pltpu.make_async_copy(src, dst, os.at[i])
        cp.start()
        return cp

    c_zg = [send(ZG + k - 1, piece, neww.at[:, y, zl, c], at_z(k)) for k in (1, 3, 2)]
    st_p = store(0, piece, neww.at[:, y, zl, c])
    st_m = store(1, momo, newm)

    ld_c.wait()
    ld_to.wait()
    for cp in c_c + c_to:
        cp.wait_recv()
    gw = SLAB // GCH

    def grad(half, j):
        return lax.dot_general(
            tbuf[half, :, pl.ds(j * gw, gw)], cbuf[...],
            (((0,), (0,)), ((), ())), preferred_element_type=F32)

    c_g = []
    for j in range(GCH):
        rows = pl.ds(j * gw, gw)
        gsend[rows] = grad(0, j).astype(BF16)
        c_g.append(send(G_ + j, gsend.at[rows], grecv.at[rows], across))

    st_p.wait()
    for cp in c_zg:
        cp.wait_recv()
    mine = neww.at[:, y, :, c]
    c_yg = [send(YG + k - 1, mine, mine, at_y(k)) for k in (1, 3, 2)]

    for cp in c_w:
        cp.wait_recv()

    @pl.loop(0, X)
    def _(k):
        rows = pl.ds(pl.multiple_of(k * TOK, TOK), TOK)
        kacc[rows] = jnp.dot(tbuf[0, rows], wbuf[0], preferred_element_type=F32)

    ld_w.wait()
    ld_tn.wait()
    for cp in c_tn:
        cp.wait_recv()
    c_k = []
    for k in (1, 3, 2, 0):
        rows = pl.ds(k * TOK, TOK)
        part = kacc[rows] + jnp.dot(tbuf[1, rows], wbuf[1], preferred_element_type=F32)
        if k:
            ksend[k - 1] = part.astype(BF16)
            c_k.append(send(K_ + k - 1, ksend.at[k - 1], krecv.at[k - 1], at_x(X - k)))
        else:
            kacc[rows] = part

    for cp in c_yg:
        cp.wait_recv()
    c_cg = send(CG, neww.at[:, :, :, c], neww.at[:, :, :, c], sibling)

    for j in range(GCH):
        gown[pl.ds(j * gw, gw)] = grad(1, j)

    for cp in c_k:
        cp.wait_recv()

    @pl.loop(0, 4)
    def _(i):
        rows = pl.ds(pl.multiple_of(i * (TOK // 4), TOK // 4), TOK // 4)
        total = kacc[rows]
        for k in range(3):
            total += krecv[k, rows].astype(F32)
        kout[rows] = total.astype(BF16)

    st_k = store(2, kout, keys)
    st_g = []
    for j in range(GCH):
        c_g[j].wait_recv()
        rows = pl.ds(j * gw, gw)
        gout[rows] = (gown[rows] + grecv[rows].astype(F32)).astype(BF16)
        st_g.append(store(3 + j, gout.at[rows], wgrad.at[rows]))
    c_cg.wait_recv()
    for cp in c_l + c_w + c_c + c_to + c_tn + c_y + c_z + c_zg + c_yg + [c_cg] + c_g + c_k:
        cp.wait_send()
    for cp in [st_m, st_k] + st_g:
        cp.wait()


def shards(tokens, inner_weight, cotangent, local_weights, anchor, momentum):
    any_space = pl.BlockSpec(memory_space=pl.ANY)
    vm = pltpu.VMEM
    keys, wgrad, neww, newm = pl.pallas_call(
        kernel,
        name="diloco_step",
        out_shape=(
            jax.ShapeDtypeStruct((TOK, KW), BF16),
            jax.ShapeDtypeStruct((SLAB, KW), BF16),
            jax.ShapeDtypeStruct((2, Y, ZL, 2, ROWS, KV), BF16),
            jax.ShapeDtypeStruct((2, ROWS, KV), F32),
        ),
        in_specs=[any_space] * 6,
        out_specs=[any_space] * 4,
        scratch_shapes=[
            vm((2, X * TOK, SLAB), BF16), vm((X * TOK, KW), BF16), vm((2, SLAB, KW), BF16),
            vm((2, Y, ZL, ROWS, KV), BF16), vm((2, Y, ZL, ROWS, KV), BF16),
            vm((2, Y, ZL, ROWS, KV), BF16), vm((3, 2, ZL, ROWS, KV), BF16),
            vm((2, ZL, ROWS, KV), BF16), vm((2, ZL, ROWS, KV), F32), vm((3, 2, ROWS, KV), BF16),
            vm((2, ROWS, KV), BF16), vm((2, ROWS, KV), F32),
            vm((2, ROWS, KV), BF16), vm((2, ROWS, KV), F32),
            vm((X * TOK, KW), F32), vm((3, TOK, KW), BF16), vm((3, TOK, KW), BF16), vm((TOK, KW), BF16),
            vm((SLAB, KW), BF16), vm((SLAB, KW), BF16), vm((SLAB, KW), F32), vm((SLAB, KW), BF16),
            pltpu.SemaphoreType.DMA((NSEM,)), pltpu.SemaphoreType.DMA((NSEM,)),
            pltpu.SemaphoreType.DMA((8,)), pltpu.SemaphoreType.DMA((3 + GCH,)),
        ],
        compiler_params=pltpu.CompilerParams(collective_id=0, has_side_effects=True),
    )(
        tokens,
        inner_weight[0],
        cotangent,
        local_weights.reshape(2, Y, ZL, 2, ROWS, KV),
        anchor.reshape(2, ROWS, KV),
        momentum.reshape(2, ROWS, KV),
    )
    return (
        keys,
        wgrad[None],
        neww.reshape(2, Y * ZL * 2 * ROWS, KV),
        newm[:, None],
    )


def solution(mesh):
    return jax.shard_map(
        shards,
        mesh=mesh,
        in_specs=(
            P(("replica", "fsdp"), None),
            P("replica", "fsdp", None),
            P(("replica", "fsdp"), None),
            P("replica", None, "fsdp", None),
            P(None, "fsdp", "replica", None),
            P(None, "fsdp", "replica", None),
        ),
        out_specs=(
            P(("replica", "fsdp"), None),
            P("replica", "fsdp", None),
            P(None, "fsdp", None),
            P(None, "fsdp", "replica", None),
        ),
        check_vma=False,
    )
```

time: 542 us -> 159 us (0.29)
  waiting for transfers between devices: 494 us -> 0 us
  Pallas kernels: 0 us -> 149 us
  matrix products: 19 us -> 0 us
  between operations: 15.7 us -> 0.64 us
  other arithmetic: 7.29 us -> 0 us
    reduce_scatter x2 -> x0, waiting for transfers between devices: 445 us -> none  [the longest x1 262 us: outer_step(): lax.psum_scatter(local_slab, 'replica', scatter_dimension=1, tiled=True)]
    pallas_call x0 -> x1, Pallas kernels: none -> 149 us  [shards(): pl.pallas_call(kernel, name='diloco_step', out_shape=(jax.ShapeDtypeStruc...]
    all_gather x2 -> x0, waiting for transfers between devices: 47.9 us -> none  [the longest x1 47.9 us: outer_step(): gathered = lax.all_gather(new_piece, 'replica', axis=1, tiled=True)]
    dot_general x2 -> x0, matrix products: 19 us -> none  [the longest x1 9.63 us: inner_pass(): lax.dot_general(columns, cotangent, (((0,), (0,)), ((), ())), preferred_e...]
    convert_element_type x1 -> x0, other arithmetic: 5.56 us -> none  [outer_step(): local_slab = local_weights[0].astype(jnp.float32)]
  transfers between devices with their start and end apart: 4 -> 0, of which waited for: 3 -> 0; matrix products, arithmetic and copies ran while one was open for 4% -> 0% of each run, Pallas kernels for 0% -> 0%
where the time goes in v1:
time: 159 us
  Pallas kernels  149 us (94%)
  local copies, waits for them, and re-layouts  8.93 us (6%)
    pallas_call x1, Pallas kernels, shards(): pl.pallas_call(kernel, name='diloco_step', out_shape=(jax.ShapeDtypeStruc...  149 us
    unnamed x6, local copies, waits for them, and re-layouts  8.93 us

profile of v1, /device:TPU:7, one launch (start us, length us, event | category | flops | bytes accessed | tf_op | source)
XLA Modules:
  0.0 158.7 jit_solution(15707455066634906132)
XLA Ops:
  0.6 149.1 %diloco_step.1 = (bf16[384,512]{1,0:T(8,128)(2,1)}, bf16[1024,512]{1,0:T(8,128)(2,1)}, bf16[2,4,4,2,32,896]{5,4,3,2,1,0:T(8,128)(2,1)}, f32[2,32,896]{2,1,0:T(8,128)}) custom-call(bf16[384,8192]{1,0:T(8,128)(2,1)} %tok.1, bf16[1024,512]{1,0:T(8,128)(2,1)} %bitcast.11, bf16[384,512]{1,0:T(8,128)(2,1)} %cot.1, bf16[2,4,4,2,32,896]{5,4,3,2,1,0:T(8,128)(2,1)} %bitcast.10, ...), custom_call_target="tpu_custom_call" | custom-call | tf_op jit(solution)/shard_map/diloco_step/pallas_call | solution.py:218
  149.7 1.8 %copy.15 = bf16[384,512]{1,0:T(8,128)(2,1)} copy(bf16[384,512]{1,0:T(8,128)(2,1)} %get-tuple-element.20) | data formatting | bytes 786432
  151.5 2.3 %copy.16 = bf16[1,1024,512]{2,1,0:T(8,128)(2,1)} copy(bf16[1,1024,512]{2,1,0:T(8,128)(2,1)} %bitcast.12) | data formatting | bytes 2097152
  153.8 0.0 copy-start
  153.8 4.2 %copy.17 = bf16[2,1024,896]{2,1,0:T(8,128)(2,1)} copy(bf16[2,1024,896]{2,1,0:T(8,128)(2,1)} %bitcast.9) | data formatting | bytes 7340032
  158.0 0.0 copy-done
  158.0 0.7 copy.18
Async XLA Ops:
  153.8 4.2 %copy-start = (f32[2,32,896]{2,1,0:T(8,128)S(1)}, f32[2,32,896]{2,1,0:T(8,128)}, u32[]{:S(2)}) copy-start(f32[2,32,896]{2,1,0:T(8,128)} %get-tuple-element.11) | copy-start | bytes 688132

commit v2 on v1

--- a/solution.py
+++ b/solution.py
@@ -19,12 +19,13 @@
 LAST_W = 1
 
 L_, W_, C_, TO, TN, YR, ZR, ZG, YG, CG, G_, K_ = (0, 2, 6, 9, 12, 15, 18, 21, 24, 27, 28, 32)
-NSEM = 35
+F_, V_ = 35, 39
+NSEM = 43
 
 
 def kernel(tok, wgt, cot, loc, anc, mom, keys, wgrad, neww, newm,
            tbuf, cbuf, wbuf, lown, lrecv, s1, s1r, s2, s2f, s2r, ancv, momv, piece, momo,
-           kacc, ksend, krecv, kout, gsend, grecv, gown, gout, ss, rs, ls, os):
+           kacc, ksend, krecv, kout, gsend, grecv, gown, gout, hop, ss, rs, ls, os):
     r = lax.axis_index("replica")
     f = lax.axis_index("fsdp")
     y, zl, c = r // 8, (r // 2) % 4, r % 2
@@ -40,12 +41,24 @@
         return (y * 8 + lax.rem(zl + k, ZL) * 2 + c, f)
 
     across = (r, x * 2 + (1 - zh))
+
+    def ring_z(k):
+        z = lax.rem(zh * ZL + zl + k, 2 * ZL)
+        return (y * 8 + lax.rem(z, ZL) * 2 + c, x * 2 + z // ZL)
+
+    def relay_to(j):
+        return ring_z(5 if j % 2 else 3)
+
+    def relay_on(j):
+        return ring_z(7 if j % 2 else 1)
+
     sibling = (y * 8 + zl * 2 + (1 - c), f)
 
     barrier = pltpu.get_barrier_semaphore()
     peers = [across, sibling]
     for k in (1, 2, 3):
         peers += [at_x(k), at_y(k), at_z(k)]
+    peers += [ring_z(k) for k in (1, 3, 5, 7)]
     for p in peers:
         pl.semaphore_signal(barrier, inc=1, device_id=p, device_id_type=MESH)
 
@@ -150,7 +163,14 @@
     for j in range(GCH):
         rows = pl.ds(j * gw, gw)
         gsend[rows] = grad(0, j).astype(BF16)
-        c_g.append(send(G_ + j, gsend.at[rows], grecv.at[rows], across))
+        c_g.append(send(G_ + j, gsend.at[rows], hop.at[rows], relay_to(j)))
+
+    c_f = []
+
+    def relay_g(j):
+        rows = pl.ds(j * gw, gw)
+        c_g[j].wait_recv()
+        c_f.append(send(F_ + j, hop.at[rows], grecv.at[rows], relay_on(j)))
 
     st_p.wait()
     for cp in c_zg:
@@ -186,6 +206,10 @@
 
     for j in range(GCH):
         gown[pl.ds(j * gw, gw)] = grad(1, j)
+        if j < 2:
+            relay_g(j)
+    for j in range(2, GCH):
+        relay_g(j)
 
     for cp in c_k:
         cp.wait_recv()
@@ -201,15 +225,31 @@
     st_k = store(2, kout, keys)
     st_g = []
     for j in range(GCH):
-        c_g[j].wait_recv()
+        c_f[j].wait_recv()
         rows = pl.ds(j * gw, gw)
         gout[rows] = (gown[rows] + grecv[rows].astype(F32)).astype(BF16)
         st_g.append(store(3 + j, gout.at[rows], wgrad.at[rows]))
     c_cg.wait_recv()
-    for cp in c_l + c_w + c_c + c_to + c_tn + c_y + c_z + c_zg + c_yg + [c_cg] + c_g + c_k:
+    for cp in c_l + c_w + c_c + c_to + c_tn + c_y + c_z + c_zg + c_yg + [c_cg] + c_g + c_f + c_k:
         cp.wait_send()
     for cp in [st_m, st_k] + st_g:
         cp.wait()
+
+
+def emit(keys, wgrad, neww, newm, keys_o, wgrad_o, neww_o, newm_o, kv, gv, wv, mv, si, so):
+    parts = [(neww.at[m, a], wv.at[m, a], neww_o.at[m, a]) for m in range(2) for a in range(Y)]
+    parts += [(wgrad.at[rows], gv.at[rows], wgrad_o.at[rows])
+              for rows in (pl.ds(0, SLAB // 2), pl.ds(SLAB // 2, SLAB // 2))]
+    parts += [(keys, kv, keys_o), (newm, mv, newm_o)]
+    loads = [pltpu.make_async_copy(a, b, si.at[i]) for i, (a, b, _) in enumerate(parts)]
+    stores = [pltpu.make_async_copy(b, o, so.at[i]) for i, (_, b, o) in enumerate(parts)]
+    for cp in loads:
+        cp.start()
+    for ld, st in zip(loads, stores):
+        ld.wait()
+        st.start()
+    for st in stores:
+        st.wait()
 
 
 def shards(tokens, inner_weight, cotangent, local_weights, anchor, momentum):
@@ -235,6 +275,7 @@
             vm((2, ROWS, KV), BF16), vm((2, ROWS, KV), F32),
             vm((X * TOK, KW), F32), vm((3, TOK, KW), BF16), vm((3, TOK, KW), BF16), vm((TOK, KW), BF16),
             vm((SLAB, KW), BF16), vm((SLAB, KW), BF16), vm((SLAB, KW), F32), vm((SLAB, KW), BF16),
+            vm((SLAB, KW), BF16),
             pltpu.SemaphoreType.DMA((NSEM,)), pltpu.SemaphoreType.DMA((NSEM,)),
             pltpu.SemaphoreType.DMA((8,)), pltpu.SemaphoreType.DMA((3 + GCH,)),
         ],
@@ -247,6 +288,15 @@
         anchor.reshape(2, ROWS, KV),
         momentum.reshape(2, ROWS, KV),
     )
+    kept = ((TOK, KW), BF16), ((SLAB, KW), BF16), ((2, Y, ZL, 2, ROWS, KV), BF16), ((2, ROWS, KV), F32)
+    keys, wgrad, neww, newm = pl.pallas_call(
+        emit,
+        name="emit_outputs",
+        out_shape=tuple(jax.ShapeDtypeStruct(*k) for k in kept),
+        in_specs=[any_space] * 4,
+        out_specs=[any_space] * 4,
+        scratch_shapes=[vm(*k) for k in kept] + [pltpu.SemaphoreType.DMA((12,))] * 2,
+    )(keys, wgrad, neww, newm)
     return (
         keys,
         wgrad[None],

time: 159 us -> 134 us (0.84)
  the two profiles are of different devices: /device:TPU:7 before, /device:TPU:36 now
where the time goes in v2:
time: 134 us
  Pallas kernels  134 us (100%)
    pallas_call x1, Pallas kernels, shards(): pl.pallas_call(kernel, name='diloco_step', out_shape=(jax.ShapeDtypeStruc...  129 us
    pallas_call x1, Pallas kernels, shards(): pl.pallas_call(emit, name='emit_outputs', out_shape=tuple((jax.ShapeDtype...  4.8 us

profile of v2, /device:TPU:36, one launch (start us, length us, event | category | flops | bytes accessed | tf_op | source)
XLA Modules:
  0.0 134.3 jit_solution(16673767414476490400)
XLA Ops:
  0.6 128.9 %diloco_step.1 = (bf16[384,512]{1,0:T(8,128)(2,1)}, bf16[1024,512]{1,0:T(8,128)(2,1)}, bf16[2,4,4,2,32,896]{5,4,3,2,1,0:T(8,128)(2,1)}, f32[2,32,896]{2,1,0:T(8,128)}) custom-call(bf16[384,8192]{1,0:T(8,128)(2,1)} %tok.1, bf16[1024,512]{1,0:T(8,128)(2,1)} %bitcast.10, bf16[384,512]{1,0:T(8,128)(2,1)} %cot.1, bf16[2,4,4,2,32,896]{5,4,3,2,1,0:T(8,128)(2,1)} %bitcast.9, ...), custom_call_target="tpu_custom_call" | custom-call | tf_op jit(solution)/shard_map/diloco_step/pallas_call | solution.py:258
  129.5 4.8 %emit_outputs.1 = (bf16[384,512]{1,0:T(8,128)(2,1)}, bf16[1024,512]{1,0:T(8,128)(2,1)}, bf16[2,4,4,2,32,896]{5,4,3,2,1,0:T(8,128)(2,1)}, f32[2,32,896]{2,1,0:T(8,128)}) custom-call(bf16[384,512]{1,0:T(8,128)(2,1)} %get-tuple-element.12.keys, bf16[1024,512]{1,0:T(8,128)(2,1)} %get-tuple-element.13.wgrad, ...), custom_call_target="tpu_custom_call" | custom-call | tf_op jit(solution)/shard_map/emit_outputs/pallas_call | solution.py:292
